TPU v7x, 32 devices: a whole 2x2x4 slice. The times are simulated.
32 devices in a mesh: grp: 2 (over x), tok: 8 (over z, y), wid: 2 (over core).
Axes of the slice: x: 2, y: 2, z: 4, core: 2. Of those that a mesh axis runs over, the one named last changes fastest.
Arguments:
- inputs: bfloat16 [128, 8192], P(('grp', 'wid'), 'tok'), may hold values from -6 to 6
- parent_gate: bfloat16 [8192, 28672], P('tok', ('grp', 'wid')), may hold values from -0.0625 to 0.0625
- parent_up: bfloat16 [8192, 28672], P('tok', ('grp', 'wid')), may hold values from -0.0625 to 0.0625
- parent_down: bfloat16 [28672, 8192], P(('grp', 'wid'), 'tok'), may hold values from -0.03125 to 0.03125
- first_gate: bfloat16 [8192, 7168], P('tok', ('grp', 'wid')), may hold values from -0.0625 to 0.0625
- first_up: bfloat16 [8192, 7168], P('tok', ('grp', 'wid')), may hold values from -0.0625 to 0.0625
- first_down: bfloat16 [7168, 8192], P(('grp', 'wid'), 'tok'), may hold values from -0.0625 to 0.0625
- second_gate: bfloat16 [8192, 5632], P('tok', ('grp', 'wid')), may hold values from -0.0625 to 0.0625
- second_up: bfloat16 [8192, 5632], P('tok', ('grp', 'wid')), may hold values from -0.0625 to 0.0625
- second_down: bfloat16 [5632, 8192], P(('grp', 'wid'), 'tok'), may hold values from -0.078125 to 0.078125
Outputs:
- target: bfloat16 [128, 8192], P(('grp', 'wid'), 'tok')
- first_error: bfloat16 [128, 8192], P(('grp', 'wid'), 'tok')
- second_error: bfloat16 [128, 8192], P(('grp', 'wid'), 'tok')
- first_grad_gate: bfloat16 [8192, 7168], P('tok', ('grp', 'wid'))
- first_grad_up: bfloat16 [8192, 7168], P('tok', ('grp', 'wid'))
- first_grad_down: bfloat16 [7168, 8192], P(('grp', 'wid'), 'tok')
- second_grad_gate: bfloat16 [8192, 5632], P('tok', ('grp', 'wid'))
- second_grad_up: bfloat16 [8192, 5632], P('tok', ('grp', 'wid'))
- second_grad_down: bfloat16 [5632, 8192], P(('grp', 'wid'), 'tok')
All inputs are finite; a program needn't handle non-finite values.
Results may differ from a plain program's by a relative error of at most 0.009.
Values may be sent and summed in bfloat16 or wider, within the bound.
A program may use at most 192 MiB of HBM per device.

v0:
```python
import jax
import jax.numpy as jnp
from jax import lax
from jax.sharding import PartitionSpec as P


def matmul(left, right):
    return jnp.dot(left, right, preferred_element_type=jnp.float32)


def inner_rows(left, right):
    return lax.dot_general(
        left, right, (((0,), (0,)), ((), ())), preferred_element_type=jnp.float32
    )


def outer_cols(left, right):
    return lax.dot_general(
        left, right, (((1,), (1,)), ((), ())), preferred_element_type=jnp.float32
    )


def body(
    inputs,
    parent_gate,
    parent_up,
    parent_down,
    first_gate,
    first_up,
    first_down,
    second_gate,
    second_up,
    second_down,
):
    columns = lax.all_gather(inputs, ("grp", "wid"), axis=0, tiled=True)
    out_rows = inputs.shape[0]
    position = lax.axis_index(("grp", "wid"))
    width_parent = parent_gate.shape[1]
    parent_both = lax.psum_scatter(
        jnp.concatenate([matmul(columns, parent_gate), matmul(columns, parent_up)], axis=1),
        "tok",
        scatter_dimension=0,
        tiled=True,
    )
    parent_hidden = (
        jax.nn.silu(parent_both[:, :width_parent]) * parent_both[:, width_parent:]
    ).astype(jnp.bfloat16)
    parent_all = lax.all_gather(parent_hidden, "tok", axis=0, tiled=True)
    target_all = lax.psum(matmul(parent_all, parent_down), ("grp", "wid")).astype(jnp.bfloat16)
    target = lax.dynamic_slice_in_dim(target_all, position * out_rows, out_rows, 0)

    def candidate(gate_w, up_w, down_w):
        width_cand = gate_w.shape[1]
        pre_both = lax.psum(
            jnp.concatenate([matmul(columns, gate_w), matmul(columns, up_w)], axis=1), "tok"
        )
        pre_gate = pre_both[:, :width_cand]
        pre_up = pre_both[:, width_cand:]
        hidden = (jax.nn.silu(pre_gate) * pre_up).astype(jnp.bfloat16)
        output_all = lax.psum(matmul(hidden, down_w), ("grp", "wid"))
        error_all = (output_all - target_all.astype(jnp.float32)).astype(jnp.bfloat16)
        error_local = lax.dynamic_slice_in_dim(error_all, position * out_rows, out_rows, 0)
        grad_down = inner_rows(hidden, error_all).astype(jnp.bfloat16)
        back_grad = lax.psum(outer_cols(error_all, down_w), "tok")
        sigmoid_gate = jax.nn.sigmoid(pre_gate)
        grad_pre_gate = (
            back_grad * pre_up * sigmoid_gate * (1.0 + pre_gate * (1.0 - sigmoid_gate))
        ).astype(jnp.bfloat16)
        grad_pre_up = (back_grad * pre_gate * sigmoid_gate).astype(jnp.bfloat16)
        grad_gate = inner_rows(columns, grad_pre_gate).astype(jnp.bfloat16)
        grad_up = inner_rows(columns, grad_pre_up).astype(jnp.bfloat16)
        return (error_local, grad_gate, grad_up, grad_down)

    first_error, first_grad_gate, first_grad_up, first_grad_down = candidate(
        first_gate, first_up, first_down
    )
    second_error, second_grad_gate, second_grad_up, second_grad_down = candidate(
        second_gate, second_up, second_down
    )
    return (
        target,
        first_error,
        second_error,
        first_grad_gate,
        first_grad_up,
        first_grad_down,
        second_grad_gate,
        second_grad_up,
        second_grad_down,
    )


def solution(mesh):
    placed = (
        P(("grp", "wid"), "tok"),
        P("tok", ("grp", "wid")),
        P("tok", ("grp", "wid")),
        P(("grp", "wid"), "tok"),
        P("tok", ("grp", "wid")),
        P("tok", ("grp", "wid")),
        P(("grp", "wid"), "tok"),
        P("tok", ("grp", "wid")),
        P("tok", ("grp", "wid")),
        P(("grp", "wid"), "tok"),
    )
    return jax.shard_map(
        body,
        mesh=mesh,
        in_specs=placed,
        out_specs=(
            P(("grp", "wid"), "tok"),
            P(("grp", "wid"), "tok"),
            P(("grp", "wid"), "tok"),
            P("tok", ("grp", "wid")),
            P("tok", ("grp", "wid")),
            P(("grp", "wid"), "tok"),
            P("tok", ("grp", "wid")),
            P("tok", ("grp", "wid")),
            P(("grp", "wid"), "tok"),
        ),
        check_vma=False,
    )
```

profile of v0, /device:TPU:0, one launch (start us, length us, event | category | flops | bytes accessed | tf_op | source)
XLA Modules:
  0.0 530.9 jit_solution(7398160950853835237)
XLA Ops:
  7.2 7.6 %all_gather.6 = bf16[128,1024]{1,0:T(8,128)(2,1)S(1)} all-gather(bf16[32,1024]{1,0:T(8,128)(2,1)} %param.10), channel_id=1, replica_groups=mesh['grp'=2,'tok'=8,'wid'=2] {'grp','wid'}, dimensions={0}, use_global_device_ids=true | all-gather | bytes 327680 | tf_op jit(solution)/shard_map/all_gather | solution.py:35
  14.8 7.4 %fusion.16 = f32[128,7168]{1,0:T(8,128)S(1)} fusion(bf16[128,1024]{1,0:T(8,128)(2,1)S(1)} %all_gather.6, bf16[1024,7168]{1,0:T(8,128)(2,1)} %param.12), kind=kOutput, calls=%fused_computation.39 | convolution fusion | flops 1879048192 | bytes 18612224 | tf_op jit(solution)/shard_map/dot_general | solution.py:8
  22.2 1.9 copy-done.1
  24.2 2.1 fusion.15
  26.3 3.4 pad_maximum_fusion
  29.8 2.6 fusion.22
  32.4 2.6 fusion.21
  37.5 1.4 pad_maximum_fusion.1
  38.9 125.1 %reduce-scatter.2.cloned.1.call-done = f32[16,14336]{1,0:T(8,128)} async-done(((f32[128,14336]{1,0:T(8,128)}), f32[16,14336]{1,0:T(8,128)}) %reduce-scatter.2.cloned.1.call-update) | async-done | bytes 917520 | tf_op jit(solution)/shard_map/reduce_scatter | solution.py:39
  164.0 2.0 fusion.6
  166.1 134.5 %all-reduce.10.cloned.1.call-done = (f32[128,3584]{1,0:T(8,128)}, f32[128,2816]{1,0:T(8,128)}) async-done(((f32[128,3584]{1,0:T(8,128)}, f32[128,2816]{1,0:T(8,128)}), (f32[128,3584]{1,0:T(8,128)}, f32[128,2816]{1,0:T(8,128)})) %all-reduce.10.cloned.1.call-update) | async-done | bytes 3276816 | tf_op jit(solution)/shard_map/psum | solution.py:54
  300.6 1.7 multiply_convert_fusion.5
  304.7 1.4 fusion.20
  306.2 42.7 %all-gather.2.cloned.1.call-done = bf16[128,7168]{1,0:T(8,128)(2,1)} async-done(((bf16[16,7168]{1,0:T(8,128)(2,1)}), bf16[128,7168]{1,0:T(8,128)(2,1)}) %all-gather.2.cloned.1.call-update) | async-done | bytes 1835024 | tf_op jit(solution)/shard_map/all_gather | solution.py:48
  348.9 8.6 %fusion.17 = f32[128,1024]{1,0:T(8,128)} fusion(bf16[128,7168]{1,0:T(8,128)(2,1)} %all-gather.2.cloned.1.call-done, bf16[7168,1024]{1,0:T(8,128)(2,1)} %param.13), kind=kOutput, calls=%fused_computation.40 | convolution fusion | flops 1879048192 | bytes 17039360 | tf_op jit(solution)/shard_map/dot_general | solution.py:8
  357.5 20.5 %all-reduce.13 = bf16[128,1024]{1,0:T(8,128)(2,1)} all-reduce(f32[128,1024]{1,0:T(8,128)} %fusion.17), channel_id=1, replica_groups=mesh['grp'=2,'tok'=8,'wid'=2] {'grp','wid'}, use_global_device_ids=true, to_apply=%region_1.2 | all-reduce | flops 131072 | bytes 786432 | tf_op jit(solution)/shard_map/psum | solution.py:49
  378.0 12.1 %all-reduce.12.cloned.1.call-done = (f32[128,1024]{1,0:T(8,128)}, f32[128,1024]{1,0:T(8,128)}) async-done(((f32[128,1024]{1,0:T(8,128)}, f32[128,1024]{1,0:T(8,128)}), (f32[128,1024]{1,0:T(8,128)}, f32[128,1024]{1,0:T(8,128)})) %all-reduce.12.cloned.1.call-update) | async-done | bytes 1048592 | tf_op jit(solution)/shard_map/psum | solution.py:60
  392.2 4.3 fusion.24
  396.5 1.9 fusion.25
  398.4 1.5 constant_dynamic-slice_fusion.2
  400.0 1.5 constant_dynamic-slice_fusion
  401.5 3.5 convolution_convert_fusion
  405.0 3.0 convolution_convert_fusion.3
  408.0 82.5 %all-reduce.8.cloned.1.call-done = (f32[128,1792]{1,0:T(8,128)}, f32[128,1408]{1,0:T(8,128)}) async-done(((f32[128,1792]{1,0:T(8,128)}, f32[128,1408]{1,0:T(8,128)}), (f32[128,1792]{1,0:T(8,128)}, f32[128,1408]{1,0:T(8,128)})) %all-reduce.8.cloned.1.call-update) | async-done | bytes 1638416 | tf_op jit(solution)/shard_map/psum | solution.py:64
  490.4 4.9 fusion.2
  495.4 3.0 fusion.3
  498.3 2.6 fusion
  500.9 2.6 fusion.1
  503.5 5.9 %copy.19 = bf16[1024,1792]{1,0:T(8,128)(2,1)} copy(bf16[1024,1792]{0,1:T(8,128)(2,1)} %fusion.2) | data formatting | bytes 7340032
  509.4 5.9 %copy.20 = bf16[1024,1792]{1,0:T(8,128)(2,1)} copy(bf16[1024,1792]{0,1:T(8,128)(2,1)} %fusion.3) | data formatting | bytes 7340032
  515.3 4.5 copy.21
  519.9 4.5 copy.22
  (45 shorter events, 7.3 us)
Async XLA Ops:
  7.2 295.1 %copy-start = (bf16[1408,1024]{1,0:T(8,128)(2,1)S(1)}, bf16[1408,1024]{1,0:T(8,128)(2,1)}, u32[]{:S(2)}) copy-start(bf16[1408,1024]{1,0:T(8,128)(2,1)} %param.19) | copy-start | bytes 8650756
  7.2 156.8 %reduce-scatter.2.cloned.1.call-start = ((), (), s32[]{:S(2)}) async-start(), calls=%async_computation.1 | async-start | bytes 8257536 | tf_op jit(solution)/shard_map/reduce_scatter | solution.py:39
  14.8 9.3 %copy-start.1 = (bf16[1024,7168]{1,0:T(8,128)(2,1)S(1)}, bf16[1024,7168]{1,0:T(8,128)(2,1)}, u32[]{:S(2)}) copy-start(bf16[1024,7168]{1,0:T(8,128)(2,1)} %param.11) | copy-start | bytes 44040196
  29.7 270.8 %all-reduce.10.cloned.1.call-start = ((), (), s32[]{:S(2)}) async-start(), calls=%async_computation.4 | async-start | bytes 6553600 | tf_op jit(solution)/shard_map/psum | solution.py:54
  29.8 5.1 copy-start.7
  32.4 3.2 copy-start.8
  38.9 310.0 %all-gather.2.cloned.1.call-start = ((), (), s32[]{:S(2)}) async-start(), calls=%async_computation.2 | async-start | bytes 2064384 | tf_op jit(solution)/shard_map/all_gather | solution.py:48
  166.0 224.0 %all-reduce.12.cloned.1.call-start = ((), (), s32[]{:S(2)}) async-start(), calls=%async_computation.5 | async-start | bytes 2097152 | tf_op jit(solution)/shard_map/psum | solution.py:60
  300.6 3.1 copy-start.5
  300.6 4.1 copy-start.2
  303.9 0.8 copy-start.3
  306.2 184.3 %all-reduce.8.cloned.1.call-start = ((), (), s32[]{:S(2)}) async-start(), calls=%async_computation.3 | async-start | bytes 3276800 | tf_op jit(solution)/shard_map/psum | solution.py:64
  391.5 0.7 copy-start.10
  391.5 5.0 copy-start.12
  398.4 6.6 %copy-start.4 = (bf16[128,1792]{1,0:T(8,128)(2,1)S(1)}, bf16[128,1792]{1,0:T(8,128)(2,1)}, u32[]{:S(2)}) copy-start(bf16[128,1792]{1,0:T(8,128)(2,1)} %copy-done.3) | copy-start | bytes 1376260
  398.4 6.6 %copy-start.11 = (bf16[128,1024]{1,0:T(8,128)(2,1)S(1)}, bf16[128,1024]{1,0:T(8,128)(2,1)}, u32[]{:S(2)}) copy-start(bf16[128,1024]{1,0:T(8,128)(2,1)} %copy-done.10) | copy-start | bytes 786436
  490.4 4.9 copy-start.6
  490.4 4.9 copy-start.13
  495.3 3.0 copy-start.9
  495.3 3.0 copy-start.14
Sparse Core Ops, SparseCore 0:
  29.9 134.1 reduce-scatter.1
  168.9 131.6 all-reduce.9
  303.3 45.4 all-gather.1
  351.7 38.2 all-reduce.11
  398.5 91.8 all-reduce.7
where the time goes:
time: 532 us; the launch traced here: 531 us
  waiting for transfers between devices  397 us (75%)
  matrix products  53 us (10%)
  blocking collectives  28.1 us (5%)
  local copies, waits for them, and re-layouts  27.4 us (5%)
  between operations  14 us (3%)
  other arithmetic  11.4 us (2%)
    psum x1, waiting for transfers between devices, candidate(): lax.psum(jnp.concatenate([matmul(columns, gate_w), matmul(columns, up_w)]...  134 us
    reduce_scatter x1, waiting for transfers between devices, body(): lax.psum_scatter(jnp.concatenate([matmul(columns, parent_gate), matmul(co...  125 us
    psum x1, waiting for transfers between devices, candidate(): back_grad = lax.psum(outer_cols(error_all, down_w), 'tok')  82.5 us
    all_gather x1, waiting for transfers between devices, body(): parent_all = lax.all_gather(parent_hidden, 'tok', axis=0, tiled=True)  42.7 us
    dot_general x9, matrix products, matmul(): return jnp.dot(left, right, preferred_element_type=jnp.float32)  27.3 us
    unnamed x34, local copies, waits for them, and re-layouts  24.4 us
    psum x1, blocking collectives, body(): lax.psum(matmul(parent_all, parent_down), ('grp', 'wid'))  20.5 us
    dot_general x6, matrix products, inner_rows(): lax.dot_general(left, right, (((0,), (0,)), ((), ())), preferred_element_...  19.5 us
  transfers between devices with their start and end apart: 5, of which 5 were waited for; matrix products, arithmetic and copies ran while one was open for 6% of the time, Pallas kernels for 0%

commit v1 on v0

v1 whole, which is shorter than its diff:
```python
import functools

import jax
import jax.numpy as jnp
from jax import lax
from jax.experimental import pallas as pl
from jax.experimental.pallas import tpu as pltpu
from jax.sharding import PartitionSpec as P

MESH = pl.DeviceIdType.MESH
LANES = 128
PIECE = 1024
VMEM_BYTES = 48 * 1024 * 1024
F32 = jnp.float32
BF16 = jnp.bfloat16


def matmul(left, right):
    return jnp.dot(left, right, preferred_element_type=F32)


def inner_rows(left, right):
    return lax.dot_general(left, right, (((0,), (0,)), ((), ())), preferred_element_type=F32)


def outer_cols(left, right):
    return lax.dot_general(left, right, (((1,), (1,)), ((), ())), preferred_element_type=F32)


def cuts(width):
    units = width // LANES
    count = -(-width // PIECE)
    ranges, at = [], 0
    for i in range(count):
        size = (units // count + (i < units % count)) * LANES
        ranges.append((at, size))
        at += size
    return ranges


def remote(src, dst, send, recv, where):
    return pltpu.make_async_remote_copy(
        src_ref=src, dst_ref=dst, send_sem=send, recv_sem=recv,
        device_id=where, device_id_type=MESH,
    )


def exchange_kernel(grid_of, widths, forward, *refs):
    na, nb = grid_of
    count = len(widths)
    per_in, per_out = (2, 1) if forward else (1, 2)
    n_in = per_in * count
    refs = list(refs)
    partial = refs[:n_in]
    del refs[:n_in]
    if forward:
        gathered = refs[:count]
        share = refs[count:3 * count]
        del refs[:3 * count]
    else:
        share = refs[:2 * count]
        gathered = refs[2 * count:4 * count]
        del refs[:4 * count]
    got1, sum1, got2, s1, r1, s2, r2, s3, r3, s4, r4 = refs

    me = lax.axis_index("tok")
    hi, lo = me // nb, lax.rem(me, nb)
    hi_peers = [lax.rem(hi + d, na) for d in range(1, na)]
    lo_peers = [lax.rem(lo + d, nb) for d in range(1, nb)]

    jobs, at = [], 0
    for k, width in enumerate(widths):
        for start, size in cuts(width):
            jobs.append((k, start, size, at))
            at += size * per_in

    barrier = pltpu.get_barrier_semaphore()
    for peer in hi_peers:
        pl.semaphore_signal(barrier, inc=1, device_id={"tok": peer * nb + lo}, device_id_type=MESH)
    for peer in lo_peers:
        pl.semaphore_signal(barrier, inc=1, device_id={"tok": hi * nb + peer}, device_id_type=MESH)
    pl.semaphore_wait(barrier, na + nb - 2)

    pending = []
    first, second, third, fourth = {}, {}, {}, {}

    for j, (k, start, size, col) in enumerate(jobs):
        first[j] = []
        for d, peer in enumerate(lo_peers):
            for i in range(per_in):
                copy = remote(
                    partial[per_in * k + i].at[:, peer, :, pl.ds(start, size)],
                    got1.at[d, :, :, pl.ds(col + i * size, size)],
                    s1.at[j, d, i], r1.at[j, d, i], {"tok": hi * nb + peer},
                )
                copy.start()
                first[j].append(copy)
        pending += first[j]

    def add_low(j):
        k, start, size, col = jobs[j]
        for copy in first[j]:
            copy.wait_recv()
        for i in range(per_in):
            cols = pl.ds(col + i * size, size)
            total = partial[per_in * k + i][:, lo, :, pl.ds(start, size)].astype(F32)
            for d in range(nb - 1):
                total = total + got1[d, :, :, cols].astype(F32)
            sum1[:, :, cols] = total.astype(BF16)
        second[j] = []
        cols = pl.ds(col, size * per_in)
        for d, peer in enumerate(hi_peers):
            copy = remote(
                sum1.at[peer, :, cols], got2.at[d, :, cols], s2.at[j, d], r2.at[j, d],
                {"tok": peer * nb + lo},
            )
            copy.start()
            second[j].append(copy)
        pending.extend(second[j])

    def add_high(j):
        k, start, size, col = jobs[j]
        for copy in second[j]:
            copy.wait_recv()
        totals = []
        for i in range(per_in):
            cols = pl.ds(col + i * size, size)
            total = partial[per_in * k + i][hi, lo, :, pl.ds(start, size)].astype(F32)
            for d in range(nb - 1):
                total = total + got1[d, hi, :, cols].astype(F32)
            for d in range(na - 1):
                total = total + got2[d, :, cols].astype(F32)
            totals.append(total)
        window = pl.ds(start, size)
        if forward:
            gate, up = totals
            share[2 * k][:, window] = gate
            share[2 * k + 1][:, window] = up
            gathered[k][hi, lo, :, window] = (gate / (1.0 + jnp.exp(-gate)) * up).astype(BF16)
            outs = [gathered[k]]
        else:
            back = totals[0]
            gate = share[2 * k][:, window]
            up = share[2 * k + 1][:, window]
            s = 1.0 / (1.0 + jnp.exp(-gate))
            outs = [gathered[2 * k], gathered[2 * k + 1]]
            outs[0][hi, lo, :, window] = (back * up * s * (1.0 + gate * (1.0 - s))).astype(BF16)
            outs[1][hi, lo, :, window] = (back * gate * s).astype(BF16)
        third[j] = []
        for d, peer in enumerate(hi_peers):
            for i, out in enumerate(outs):
                here = out.at[hi, lo, :, window]
                copy = remote(
                    here, here, s3.at[j, d, i], r3.at[j, d, i], {"tok": peer * nb + lo}
                )
                copy.start()
                third[j].append(copy)
        pending.extend(third[j])

    def spread_low(j):
        k, start, size, col = jobs[j]
        for copy in third[j]:
            copy.wait_recv()
        outs = [gathered[per_out * k + i] for i in range(per_out)]
        fourth[j] = []
        for d, peer in enumerate(lo_peers):
            for i, out in enumerate(outs):
                here = out.at[:, lo, :, pl.ds(start, size)]
                copy = remote(
                    here, here, s4.at[j, d, i], r4.at[j, d, i], {"tok": hi * nb + peer}
                )
                copy.start()
                fourth[j].append(copy)
        pending.extend(fourth[j])

    total_jobs = len(jobs)
    for step in range(total_jobs + 2):
        if step < total_jobs:
            add_low(step)
        if 0 <= step - 1 < total_jobs:
            add_high(step - 1)
        if 0 <= step - 2 < total_jobs:
            spread_low(step - 2)
    for j in range(total_jobs):
        for copy in fourth[j]:
            copy.wait_recv()
    for copy in pending:
        copy.wait_send()


def exchange(arrays, shares, tok, forward, ident):
    na = 4 if tok % 4 == 0 else 1
    nb = tok // na
    per_in, per_out = (2, 1) if forward else (1, 2)
    count = len(arrays) // per_in
    tokens = arrays[0].shape[0]
    rows = tokens // tok
    real = [x.shape[1] for x in arrays]
    arrays = [jnp.pad(x, ((0, 0), (0, -x.shape[1] % LANES))) for x in arrays]
    widths = [arrays[per_in * k].shape[1] for k in range(count)]
    all_cols = per_in * sum(widths)
    n_jobs = sum(len(cuts(w)) for w in widths)
    gathered = [
        jax.ShapeDtypeStruct((na, nb, rows, w), BF16) for w in widths for _ in range(per_out)
    ]
    kept = [jax.ShapeDtypeStruct((rows, w), F32) for w in widths for _ in range(2)]
    lead = max(nb - 1, 1)
    dma = pltpu.SemaphoreType.DMA
    scratch = [
        pltpu.VMEM((lead, na, rows, all_cols), BF16),
        pltpu.VMEM((na, rows, all_cols), BF16),
        pltpu.VMEM((max(na - 1, 1), rows, all_cols), BF16),
        dma((n_jobs, lead, per_in)), dma((n_jobs, lead, per_in)),
        dma((n_jobs, max(na - 1, 1))), dma((n_jobs, max(na - 1, 1))),
        dma((n_jobs, max(na - 1, 1), per_out)), dma((n_jobs, max(na - 1, 1), per_out)),
        dma((n_jobs, lead, per_out)), dma((n_jobs, lead, per_out)),
    ]
    outs = gathered + kept if forward else gathered
    vmem = pl.BlockSpec(memory_space=pltpu.VMEM)
    operands = [x.reshape(na, nb, rows, x.shape[1]) for x in arrays] + list(shares)
    results = pl.pallas_call(
        functools.partial(exchange_kernel, (na, nb), widths, forward),
        out_shape=outs,
        in_specs=[vmem] * len(operands),
        out_specs=[vmem] * len(outs),
        scratch_shapes=scratch,
        compiler_params=pltpu.CompilerParams(
            collective_id=ident, has_side_effects=True, vmem_limit_bytes=VMEM_BYTES
        ),
        name="forward_exchange" if forward else "backward_exchange",
    )(*operands)
    full = [
        x.reshape(tokens, x.shape[-1])[:, : real[i * per_in // per_out]]
        for i, x in enumerate(results[: len(gathered)])
    ]
    return full, results[len(gathered):]


def hidden_group(sizes):
    ngrp, nwid = sizes
    total = ngrp * nwid
    me = lax.axis_index("grp") * nwid + lax.axis_index("wid")
    peers = [lax.rem(me + d, total) for d in range(1, total)]
    places = [{"grp": p // nwid, "wid": lax.rem(p, nwid)} for p in peers]
    barrier = pltpu.get_barrier_semaphore()
    for place in places:
        pl.semaphore_signal(barrier, inc=1, device_id=place, device_id_type=MESH)
    pl.semaphore_wait(barrier, total - 1)
    return me, peers, places


def gather_kernel(sizes, x_ref, out_ref, own, send, recv):
    me, peers, places = hidden_group(sizes)
    copies = []
    for d, place in enumerate(places):
        copy = remote(x_ref, out_ref.at[me], send.at[d], recv.at[d], place)
        copy.start()
        copies.append(copy)
    local = pltpu.make_async_copy(x_ref, out_ref.at[me], own)
    local.start()
    local.wait()
    for copy in copies:
        copy.wait()


def gather_rows(x, sizes):
    total = sizes[0] * sizes[1]
    vmem = pl.BlockSpec(memory_space=pltpu.VMEM)
    dma = pltpu.SemaphoreType.DMA
    out = pl.pallas_call(
        functools.partial(gather_kernel, sizes),
        out_shape=jax.ShapeDtypeStruct((total,) + x.shape, x.dtype),
        in_specs=[vmem],
        out_specs=vmem,
        scratch_shapes=[dma, dma((total - 1,)), dma((total - 1,))],
        compiler_params=pltpu.CompilerParams(collective_id=0, has_side_effects=True),
        name="gather_rows",
    )(x)
    return out.reshape(total * x.shape[0], x.shape[1])


def errors_kernel(
    sizes, t_ref, a_ref, b_ref, target, a_err, b_err, a_all, b_all, got, s1, r1, s2, r2
):
    me, peers, places = hidden_group(sizes)
    sources = (t_ref, a_ref, b_ref)
    copies = []
    for i, source in enumerate(sources):
        for d, (peer, place) in enumerate(zip(peers, places)):
            copy = remote(source.at[peer], got.at[d, i], s1.at[d, i], r1.at[d, i], place)
            copy.start()
            copies.append(copy)
    for copy in copies:
        copy.wait_recv()
    totals = []
    for i, source in enumerate(sources):
        total = source[me].astype(F32)
        for d in range(len(peers)):
            total = total + got[d, i].astype(F32)
        totals.append(total)
    goal = totals[0].astype(BF16)
    target[...] = goal
    goal = goal.astype(F32)
    sends = []
    for i, (total, own, full) in enumerate(
        ((totals[1], a_err, a_all), (totals[2], b_err, b_all))
    ):
        value = (total - goal).astype(BF16)
        own[...] = value
        full[me] = value
        for d, place in enumerate(places):
            copy = remote(full.at[me], full.at[me], s2.at[d, i], r2.at[d, i], place)
            copy.start()
            sends.append(copy)
    for copy in sends:
        copy.wait_recv()
    for copy in copies + sends:
        copy.wait_send()


def errors(parts, sizes):
    total = sizes[0] * sizes[1]
    tokens, features = parts[0].shape
    rows = tokens // total
    vmem = pl.BlockSpec(memory_space=pltpu.VMEM)
    dma = pltpu.SemaphoreType.DMA
    own = jax.ShapeDtypeStruct((rows, features), BF16)
    full = jax.ShapeDtypeStruct((total, rows, features), BF16)
    target, a_err, b_err, a_all, b_all = pl.pallas_call(
        functools.partial(errors_kernel, sizes),
        out_shape=[own, own, own, full, full],
        in_specs=[vmem] * 3,
        out_specs=[vmem] * 5,
        scratch_shapes=[
            pltpu.VMEM((total - 1, 3, rows, features), BF16),
            dma((total - 1, 3)), dma((total - 1, 3)), dma((total - 1, 2)), dma((total - 1, 2)),
        ],
        compiler_params=pltpu.CompilerParams(
            collective_id=1, has_side_effects=True, vmem_limit_bytes=VMEM_BYTES
        ),
        name="errors",
    )(*[x.reshape(total, rows, features) for x in parts])
    return target, a_err, b_err, a_all.reshape(tokens, -1), b_all.reshape(tokens, -1)


def outer_kernel(left, gate, up, gate_out, up_out):
    gate_out[...] = matmul(left[...], gate[...]).astype(BF16)
    up_out[...] = matmul(left[...], up[...]).astype(BF16)


def weight_grads(columns_t, gate, up):
    features, tokens = columns_t.shape
    width = gate.shape[1]
    tile = next((t for t in (256, LANES) if width % t == 0), width)
    block = pl.BlockSpec((tokens, tile), lambda i: (0, i))
    out_block = pl.BlockSpec((features, tile), lambda i: (0, i))
    out = jax.ShapeDtypeStruct((features, width), BF16)
    return pl.pallas_call(
        outer_kernel,
        grid=(width // tile,),
        out_shape=[out, out],
        in_specs=[pl.BlockSpec((features, tokens), lambda i: (0, 0)), block, block],
        out_specs=[out_block, out_block],
        compiler_params=pltpu.CompilerParams(vmem_limit_bytes=VMEM_BYTES),
        cost_estimate=pl.CostEstimate(
            flops=4 * features * tokens * width,
            bytes_accessed=4 * (features + tokens) * width,
            transcendentals=0,
        ),
        name="weight_grads",
    )(columns_t, gate, up)


def body(
    tok, sizes, inputs, parent_gate, parent_up, parent_down, first_gate, first_up, first_down,
    second_gate, second_up, second_down,
):
    columns = gather_rows(inputs, sizes)
    weights = (parent_gate, parent_up, first_gate, first_up, second_gate, second_up)
    partials = [matmul(columns, w).astype(BF16) for w in weights]
    (parent_hidden, first_hidden, second_hidden), kept = exchange(partials, (), tok, True, 2)
    outs = [
        matmul(parent_hidden, parent_down).astype(BF16),
        matmul(first_hidden, first_down).astype(BF16),
        matmul(second_hidden, second_down).astype(BF16),
    ]
    target, first_error, second_error, first_all, second_all = errors(outs, sizes)
    backs = [
        outer_cols(first_all, first_down).astype(BF16),
        outer_cols(second_all, second_down).astype(BF16),
    ]
    grads, _ = exchange(backs, kept[2:], tok, False, 3)
    first_grad_down = inner_rows(first_hidden, first_all).astype(BF16)
    second_grad_down = inner_rows(second_hidden, second_all).astype(BF16)
    columns_t = columns.T
    first_grad_gate, first_grad_up = weight_grads(columns_t, grads[0], grads[1])
    second_grad_gate, second_grad_up = weight_grads(columns_t, grads[2], grads[3])
    return (
        target, first_error, second_error,
        first_grad_gate, first_grad_up, first_grad_down,
        second_grad_gate, second_grad_up, second_grad_down,
    )


def solution(mesh):
    tok = mesh.shape["tok"]
    sizes = (mesh.shape["grp"], mesh.shape["wid"])
    rows = P(("grp", "wid"), "tok")
    cols = P("tok", ("grp", "wid"))
    return jax.shard_map(
        functools.partial(body, tok, sizes),
        mesh=mesh,
        in_specs=(rows, cols, cols, rows, cols, cols, rows, cols, cols, rows),
        out_specs=(rows, rows, rows, cols, cols, rows, cols, cols, rows),
        check_vma=False,
    )
```

time: 532 us -> 235 us (0.44)
  waiting for transfers between devices: 397 us -> 0 us
  Pallas kernels: 0 us -> 189 us
  blocking collectives: 28.1 us -> 0 us
  matrix products: 53 us -> 33.5 us
  local copies, waits for them, and re-layouts: 27.4 us -> 10.5 us
  between operations: 14 us -> 0.91 us
  other arithmetic: 11.4 us -> 0 us
    psum x3 -> x0, waiting for transfers between devices: 229 us -> none  [the longest x1 134 us: candidate(): lax.psum(jnp.concatenate([matmul(columns, gate_w), matmul(columns, up_w)]...]
    pallas_call x0 -> x6, Pallas kernels: none -> 189 us  [the longest x2 151 us: exchange(): pl.pallas_call(functools.partial(exchange_kernel, (na, nb), widths, forwa...]
    reduce_scatter x1 -> x0, waiting for transfers between devices: 125 us -> none  [body(): lax.psum_scatter(jnp.concatenate([matmul(columns, parent_gate), matmul(co...]
    all_gather x1 -> x0, waiting for transfers between devices: 42.7 us -> none  [body(): parent_all = lax.all_gather(parent_hidden, 'tok', axis=0, tiled=True)]
    psum x1 -> x0, blocking collectives: 20.5 us -> none  [body(): lax.psum(matmul(parent_all, parent_down), ('grp', 'wid'))]
    unnamed x34 -> x53, local copies, waits for them, and re-layouts: 24.4 us -> 8.73 us
    dot_general x6 -> x2, matrix products: 19.5 us -> 5.49 us  [inner_rows(): lax.dot_general(left, right, (((0,), (0,)), ((), ())), preferred_element_...]
    all_gather x1 -> x0, blocking collectives: 7.57 us -> none  [body(): columns = lax.all_gather(inputs, ('grp', 'wid'), axis=0, tiled=True)]
  transfers between devices with their start and end apart: 5 -> 0, of which waited for: 5 -> 0; matrix products, arithmetic and copies ran while one was open for 6% -> 0% of each run, Pallas kernels for 0% -> 0%
where the time goes in v1:
time: 235 us; the launch traced here: 234 us
  Pallas kernels  189 us (80%)
  matrix products  33.5 us (14%)
  local copies, waits for them, and re-layouts  10.5 us (4%)
    pallas_call x2, Pallas kernels, exchange(): pl.pallas_call(functools.partial(exchange_kernel, (na, nb), widths, forwa...  151 us
    dot_general x9, matrix products, matmul(): return jnp.dot(left, right, preferred_element_type=F32)  23.4 us
    pallas_call x1, Pallas kernels, errors(): pl.pallas_call(functools.partial(errors_kernel, sizes), out_shape=[own, o...  17.9 us
    pallas_call x2, Pallas kernels, weight_grads(): pl.pallas_call(outer_kernel, grid=(width // tile,), out_shape=[out, out],...  12.1 us
    unnamed x53, local copies, waits for them, and re-layouts  8.73 us
    pallas_call x1, Pallas kernels, gather_rows(): pl.pallas_call(functools.partial(gather_kernel, sizes), out_shape=jax.Sha...  8.05 us
    dot_general x2, matrix products, inner_rows(): lax.dot_general(left, right, (((0,), (0,)), ((), ())), preferred_element_...  5.49 us

profile of v1, /device:TPU:0, one launch (start us, length us, event | category | flops | bytes accessed | tf_op | source)
XLA Modules:
  0.0 233.9 jit_solution(6910417426319485525)
XLA Ops:
  0.7 8.1 %gather_rows.1 = bf16[4,32,1024]{2,1,0:T(8,128)(2,1)} custom-call(bf16[32,1024]{1,0:T(8,128)(2,1)} %x_ref.1), custom_call_target="tpu_custom_call" | custom-call | tf_op jit(solution)/shard_map/gather_rows/pallas_call | solution.py:270
  8.7 8.7 %convolution_convert_fusion.1 = bf16[128,7168]{1,0:T(8,128)(2,1)} fusion(bf16[128,1024]{1,0:T(8,128)(2,1)} %bitcast.72, bf16[1024,7168]{1,0:T(8,128)(2,1)} %param.11), kind=kOutput, calls=%fused_computation.1 | convolution fusion | flops 1879965696 | bytes 16777216 | tf_op jit(solution)/shard_map/dot_general | solution.py:19
  17.5 1.4 copy-done.18
  18.8 3.4 %convolution_convert_fusion = bf16[128,7168]{1,0:T(8,128)(2,1)} fusion(bf16[128,1024]{1,0:T(8,128)(2,1)S(1)} %bitcast.74, bf16[1024,7168]{1,0:T(8,128)(2,1)S(1)} %copy-done.18), kind=kOutput, calls=%fused_computation | convolution fusion | flops 1879965696 | bytes 16777216 | tf_op jit(solution)/shard_map/dot_general | solution.py:19
  22.2 0.7 convolution_convert_fusion.6
  22.8 1.4 copy-done.22
  24.2 0.7 convolution_convert_fusion.5
  24.9 0.2 copy-done.23
  25.1 0.6 convolution_convert_fusion.9
  25.7 0.5 copy-done.24
  26.2 0.6 convolution_convert_fusion.8
  26.8 109.5 %forward_exchange.1 = (bf16[4,2,16,7168]{3,2,1,0:T(8,128)(2,1)S(1)}, bf16[4,2,16,1792]{3,2,1,0:T(8,128)(2,1)S(1)}, bf16[4,2,16,1408]{3,2,1,0:T(8,128)(2,1)S(1)},...) custom-call(bf16[4,2,16,7168]{3,2,1,0:T(8,128)(2,1)} %bitcast.79, ...), custom_call_target="tpu_custom_call" | custom-call | tf_op jit(solution)/shard_map/forward_exchange/pallas_call | solution.py:221
  136.4 7.6 %convolution_convert_fusion.12 = bf16[128,1024]{1,0:T(8,128)(2,1)S(1)} fusion(bf16[128,7168]{1,0:T(8,128)(2,1)S(1)} %bitcast.48, bf16[7168,1024]{1,0:T(8,128)(2,1)} %param.13), kind=kOutput, calls=%fused_computation.12 | convolution fusion | flops 1879179264 | bytes 16777216 | tf_op jit(solution)/shard_map/dot_general | solution.py:19
  144.0 0.7 convolution_convert_fusion.10
  144.7 0.6 convolution_convert_fusion.11
  145.3 17.9 %errors.1 = (bf16[32,1024]{1,0:T(8,128)(2,1)S(1)}, bf16[32,1024]{1,0:T(8,128)(2,1)S(1)}, bf16[32,1024]{1,0:T(8,128)(2,1)S(1)}, bf16[4,32,1024]{2,1,0:T(8,128)(2,1)S(1)}, bf16[4,32,1024]{2,1,0:T(8,128)(2,1)S(1)}) custom-call(bf16[4,32,1024]{2,1,0:T(8,128)(2,1)S(1)} %bitcast.59, bf16[4,32,1024]{2,1,0:T(8,128)(2,1)S(1)} %bitcast.62, ...), custom_call_target="tpu_custom_call" | custom-call | tf_op jit(solution)/shard_map/errors/pallas_call | solution.py:329
  163.2 0.7 copy-done.3
  163.9 0.7 copy-done.5
  164.6 0.6 copy-done.12
  165.2 0.6 copy-done.14
  165.9 0.6 copy-done.16
  166.5 1.8 copy.20
  168.3 3.5 %convolution_convert_fusion.4 = bf16[128,1792]{1,0:T(8,128)(2,1)S(1)} fusion(bf16[128,1024]{1,0:T(8,128)(2,1)} %bitcast.60, bf16[1792,1024]{1,0:T(8,128)(2,1)} %param.16), kind=kOutput, calls=%fused_computation.4 | convolution fusion | flops 469991424 | bytes 4390912 | tf_op jit(solution)/shard_map/dot_general | solution.py:27
  171.8 1.0 convolution_convert_fusion.7
  172.9 41.5 %backward_exchange.1 = (bf16[4,2,16,1792]{3,2,1,0:T(8,128)(2,1)S(1)}, bf16[4,2,16,1792]{3,2,1,0:T(8,128)(2,1)S(1)}, bf16[4,2,16,1408]{3,2,1,0:T(8,128)(2,1)S(1)}, bf16[4,2,16,1408]{3,2,1,0:T(8,128)(2,1)S(1)}) custom-call(bf16[4,2,16,1792]{3,2,1,0:T(8,128)(2,1)S(1)} %bitcast.51, bf16[4,2,16,1408]{3,2,1,0:T(8,128)(2,1)S(1)} %bitcast.54, ...), custom_call_target="tpu_custom_call" | custom-call | tf_op jit(solution)/shard_map/backward_exchange/pallas_call | solution.py:221
  214.4 5.6 %weight_grads.2 = (bf16[1024,1792]{1,0:T(8,128)(2,1)}, bf16[1024,1792]{1,0:T(8,128)(2,1)}) custom-call(bf16[1024,128]{1,0:T(8,128)(2,1)S(1)} %bitcast.66, bf16[128,1792]{1,0:T(8,128)(2,1)S(1)} %bitcast.68, bf16[128,1792]{1,0:T(8,128)(2,1)S(1)} %bitcast.69), custom_call_target="tpu_custom_call" | custom-call | flops 939524096 | bytes 8257536 | tf_op jit(solution)/shard_map/weight_grads/pallas_call | solution.py:358
  220.0 3.0 %convolution_convert_fusion.3 = bf16[1792,1024]{1,0:T(8,128)(2,1)} fusion(bf16[128,1792]{1,0:T(8,128)(2,1)S(1)} %bitcast.50, bf16[128,1024]{1,0:T(8,128)(2,1)S(1)} %bitcast.61), kind=kOutput, calls=%fused_computation.3 | convolution fusion | flops 471597056 | bytes 4390912 | tf_op jit(solution)/shard_map/dot_general | solution.py:23
  223.0 6.5 %weight_grads.3 = (bf16[1024,1408]{1,0:T(8,128)(2,1)}, bf16[1024,1408]{1,0:T(8,128)(2,1)}) custom-call(bf16[1024,128]{1,0:T(8,128)(2,1)S(1)} %bitcast.67, bf16[128,1408]{1,0:T(8,128)(2,1)S(1)} %bitcast.70, bf16[128,1408]{1,0:T(8,128)(2,1)S(1)} %bitcast.71), custom_call_target="tpu_custom_call" | custom-call | flops 738197504 | bytes 6488064 | tf_op jit(solution)/shard_map/weight_grads/pallas_call | solution.py:358
  229.5 2.5 %convolution_convert_fusion.2 = bf16[1408,1024]{1,0:T(8,128)(2,1)} fusion(bf16[128,1408]{1,0:T(8,128)(2,1)S(1)} %bitcast.56, bf16[128,1024]{1,0:T(8,128)(2,1)S(1)} %bitcast.65), kind=kOutput, calls=%fused_computation.2 | convolution fusion | flops 370540544 | bytes 3506176 | tf_op jit(solution)/shard_map/dot_general | solution.py:23
  232.0 0.6 copy.24
  232.6 0.6 copy.25
  233.3 0.6 copy.26
  (41 shorter events, 0.1 us)
Async XLA Ops:
  0.6 144.1 %copy-start = (bf16[1408,1024]{1,0:T(8,128)(2,1)S(1)}, bf16[1408,1024]{1,0:T(8,128)(2,1)}, u32[]{:S(2)}) copy-start(bf16[1408,1024]{1,0:T(8,128)(2,1)} %param.19) | copy-start | bytes 8650756
  8.7 10.1 %copy-start.18 = (bf16[1024,7168]{1,0:T(8,128)(2,1)S(1)}, bf16[1024,7168]{1,0:T(8,128)(2,1)}, u32[]{:S(2)}) copy-start(bf16[1024,7168]{1,0:T(8,128)(2,1)} %param.12) | copy-start | bytes 44040196
  8.7 10.1 %copy-start.19 = (bf16[4,32,1024]{2,1,0:T(8,128)(2,1)S(1)}, bf16[4,32,1024]{2,1,0:T(8,128)(2,1)}, u32[]{:S(2)}) copy-start(bf16[4,32,1024]{2,1,0:T(8,128)(2,1)} %gather_rows.1) | copy-start | bytes 786436
  18.8 3.4 %copy-start.21 = (bf16[1024,1792]{1,0:T(8,128)(2,1)S(1)}, bf16[1024,1792]{1,0:T(8,128)(2,1)}, u32[]{:S(2)}) copy-start(bf16[1024,1792]{1,0:T(8,128)(2,1)} %param.14) | copy-start | bytes 11010052
  22.2 2.0 copy-start.22
  22.2 2.9 %copy-start.23 = (bf16[1024,1408]{1,0:T(8,128)(2,1)S(1)}, bf16[1024,1408]{1,0:T(8,128)(2,1)}, u32[]{:S(2)}) copy-start(bf16[1024,1408]{1,0:T(8,128)(2,1)} %param.17) | copy-start | bytes 8650756
  24.2 2.0 copy-start.24
  136.3 7.7 %copy-start.8 = (f32[16,1792]{1,0:T(8,128)}, f32[16,1792]{1,0:T(8,128)S(1)}, u32[]{:S(2)}) copy-start(f32[16,1792]{1,0:T(8,128)S(1)} %get-tuple-element.38.refs_3_) | copy-start | bytes 344068
  136.3 7.7 %copy-start.10 = (f32[16,1408]{1,0:T(8,128)}, f32[16,1408]{1,0:T(8,128)S(1)}, u32[]{:S(2)}) copy-start(f32[16,1408]{1,0:T(8,128)S(1)} %get-tuple-element.40.refs_5_) | copy-start | bytes 270340
  136.3 8.4 %copy-start.1 = (bf16[4,2,16,1408]{3,2,1,0:T(8,128)(2,1)}, bf16[4,2,16,1408]{3,2,1,0:T(8,128)(2,1)S(1)}, u32[]{:S(2)}) copy-start(bf16[4,2,16,1408]{3,2,1,0:T(8,128)(2,1)S(1)} %get-tuple-element.31) | copy-start | bytes 1081348
  136.3 7.6 %copy-start.20 = (bf16[1792,1024]{1,0:T(8,128)(2,1)S(1)}, bf16[1792,1024]{1,0:T(8,128)(2,1)}, u32[]{:S(2)}) copy-start(bf16[1792,1024]{1,0:T(8,128)(2,1)} %param.16) | copy-start | bytes 11010052
  163.2 0.7 copy-start.3
  163.9 0.7 copy-start.5
  164.6 0.6 copy-start.12
  165.2 0.6 copy-start.14
  165.9 0.6 copy-start.16
  168.3 3.5 %copy-start.6 = (bf16[4,32,1024]{2,1,0:T(8,128)(2,1)S(1)}, bf16[4,32,1024]{2,1,0:T(8,128)(2,1)}, u32[]{:S(2)}) copy-start(bf16[4,32,1024]{2,1,0:T(8,128)(2,1)} %copy-done.5) | copy-start | bytes 786436
  168.3 4.6 %copy-start.9 = (f32[16,1792]{1,0:T(8,128)S(1)}, f32[16,1792]{1,0:T(8,128)}, u32[]{:S(2)}) copy-start(f32[16,1792]{1,0:T(8,128)} %copy-done.8) | copy-start | bytes 344068
  168.3 4.6 %copy-start.11 = (f32[16,1408]{1,0:T(8,128)S(1)}, f32[16,1408]{1,0:T(8,128)}, u32[]{:S(2)}) copy-start(f32[16,1408]{1,0:T(8,128)} %copy-done.10) | copy-start | bytes 270340
  168.3 46.2 %copy-start.7 = (bf16[128,1024]{0,1:T(8,128)(2,1)S(1)}, bf16[128,1024]{0,1:T(8,128)(2,1)}, u32[]{:S(2)}) copy-start(bf16[128,1024]{0,1:T(8,128)(2,1)} %copy.20) | copy-start | bytes 786436
  171.8 48.2 %copy-start.4 = (bf16[4,32,1024]{2,1,0:T(8,128)(2,1)S(1)}, bf16[4,32,1024]{2,1,0:T(8,128)(2,1)}, u32[]{:S(2)}) copy-start(bf16[4,32,1024]{2,1,0:T(8,128)(2,1)} %copy-done.3) | copy-start | bytes 786436
  220.0 9.5 %copy-start.2 = (bf16[4,2,16,1408]{3,2,1,0:T(8,128)(2,1)S(1)}, bf16[4,2,16,1408]{3,2,1,0:T(8,128)(2,1)}, u32[]{:S(2)}) copy-start(bf16[4,2,16,1408]{3,2,1,0:T(8,128)(2,1)} %copy-done.1) | copy-start | bytes 1081348
  223.0 9.0 %copy-start.17 = (bf16[32,1024]{1,0:T(8,128)(2,1)S(1)}, bf16[32,1024]{1,0:T(8,128)(2,1)}, u32[]{:S(2)}) copy-start(bf16[32,1024]{1,0:T(8,128)(2,1)} %copy-done.16) | copy-start | bytes 196612
  223.0 9.6 %copy-start.15 = (bf16[32,1024]{1,0:T(8,128)(2,1)S(1)}, bf16[32,1024]{1,0:T(8,128)(2,1)}, u32[]{:S(2)}) copy-start(bf16[32,1024]{1,0:T(8,128)(2,1)} %copy-done.14) | copy-start | bytes 196612
  223.0 10.3 %copy-start.13 = (bf16[32,1024]{1,0:T(8,128)(2,1)S(1)}, bf16[32,1024]{1,0:T(8,128)(2,1)}, u32[]{:S(2)}) copy-start(bf16[32,1024]{1,0:T(8,128)(2,1)} %copy-done.12) | copy-start | bytes 196612

commit v2 on v1

--- a/solution.py
+++ b/solution.py
@@ -10,7 +10,8 @@
 MESH = pl.DeviceIdType.MESH
 LANES = 128
 PIECE = 1024
-VMEM_BYTES = 48 * 1024 * 1024
+MIB = 1024 * 1024
+SLOTS = 4
 F32 = jnp.float32
 BF16 = jnp.bfloat16
 
@@ -49,10 +50,16 @@
     na, nb = grid_of
     count = len(widths)
     per_in, per_out = (2, 1) if forward else (1, 2)
-    n_in = per_in * count
     refs = list(refs)
-    partial = refs[:n_in]
-    del refs[:n_in]
+    if forward:
+        left, weights = refs[0], refs[1:3]
+        partial = [refs[-4], refs[-3]] + refs[3:2 * count + 1]
+        held, loaded = refs[-2], refs[-1]
+        del refs[:2 * count + 1]
+        del refs[-4:]
+    else:
+        partial = refs[:count]
+        del refs[:count]
     if forward:
         gathered = refs[:count]
         share = refs[count:3 * count]
@@ -69,10 +76,27 @@
     lo_peers = [lax.rem(lo + d, nb) for d in range(1, nb)]
 
     jobs, at = [], 0
-    for k, width in enumerate(widths):
-        for start, size in cuts(width):
+    order = list(range(1, count)) + [0] if forward else list(range(count))
+    for k in order:
+        for start, size in cuts(widths[k]):
             jobs.append((k, start, size, at))
             at += size * per_in
+    made = [j for j, job in enumerate(jobs) if forward and job[0] == 0]
+
+    def load(n):
+        k, start, size, col = jobs[made[n]]
+        return [
+            pltpu.make_async_copy(
+                weights[i].at[:, pl.ds(start, size)],
+                held.at[n % SLOTS, i, :, pl.ds(0, size)],
+                loaded.at[n % SLOTS, i],
+            )
+            for i in range(2)
+        ]
+
+    for n in range(min(SLOTS, len(made))):
+        for copy in load(n):
+            copy.start()
 
     barrier = pltpu.get_barrier_semaphore()
     for peer in hi_peers:
@@ -84,7 +108,19 @@
     pending = []
     first, second, third, fourth = {}, {}, {}, {}
 
-    for j, (k, start, size, col) in enumerate(jobs):
+    def send_low(j):
+        k, start, size, col = jobs[j]
+        if j in made:
+            n = made.index(j)
+            for i, copy in enumerate(load(n)):
+                copy.wait()
+                product = matmul(left[...], held[n % SLOTS, i, :, pl.ds(0, size)]).astype(BF16)
+                partial[i][:, :, :, pl.ds(start, size)] = product.reshape(
+                    na, nb, left.shape[0] // (na * nb), size
+                )
+            if n + SLOTS < len(made):
+                for copy in load(n + SLOTS):
+                    copy.start()
         first[j] = []
         for d, peer in enumerate(lo_peers):
             for i in range(per_in):
@@ -95,7 +131,7 @@
                 )
                 copy.start()
                 first[j].append(copy)
-        pending += first[j]
+        pending.extend(first[j])
 
     def add_low(j):
         k, start, size, col = jobs[j]
@@ -174,7 +210,12 @@
         pending.extend(fourth[j])
 
     total_jobs = len(jobs)
+    ahead = total_jobs - len(made) + 1 if made else total_jobs
+    for j in range(min(ahead, total_jobs)):
+        send_low(j)
     for step in range(total_jobs + 2):
+        if step + ahead < total_jobs:
+            send_low(step + ahead)
         if step < total_jobs:
             add_low(step)
         if 0 <= step - 1 < total_jobs:
@@ -188,16 +229,22 @@
         copy.wait_send()
 
 
-def exchange(arrays, shares, tok, forward, ident):
+def padded(x):
+    return jnp.pad(x, ((0, 0), (0, -x.shape[1] % LANES)))
+
+
+def exchange(arrays, shares, tok, forward, ident, product=()):
     na = 4 if tok % 4 == 0 else 1
     nb = tok // na
     per_in, per_out = (2, 1) if forward else (1, 2)
-    count = len(arrays) // per_in
     tokens = arrays[0].shape[0]
     rows = tokens // tok
-    real = [x.shape[1] for x in arrays]
-    arrays = [jnp.pad(x, ((0, 0), (0, -x.shape[1] % LANES))) for x in arrays]
-    widths = [arrays[per_in * k].shape[1] for k in range(count)]
+    real = [x.shape[1] for x in tuple(product[1:]) + tuple(arrays)]
+    product = list(product[:1]) + [padded(x) for x in product[1:]]
+    arrays = [padded(x) for x in arrays]
+    all_widths = [x.shape[1] for x in product[1:] + arrays]
+    widths = all_widths[::per_in]
+    count = len(widths)
     all_cols = per_in * sum(widths)
     n_jobs = sum(len(cuts(w)) for w in widths)
     gathered = [
@@ -217,15 +264,24 @@
     ]
     outs = gathered + kept if forward else gathered
     vmem = pl.BlockSpec(memory_space=pltpu.VMEM)
-    operands = [x.reshape(na, nb, rows, x.shape[1]) for x in arrays] + list(shares)
+    in_specs = [vmem] * (len(arrays) + len(shares))
+    if forward:
+        piece = max(size for _, size in cuts(widths[0]))
+        scratch += [pltpu.VMEM((na, nb, rows, widths[0]), BF16)] * 2
+        scratch += [
+            pltpu.VMEM((SLOTS, 2, product[0].shape[1], piece), BF16), dma((SLOTS, 2)),
+        ]
+        in_specs = [vmem] + [pl.BlockSpec(memory_space=pl.ANY)] * 2 + in_specs
+    operands = product + [x.reshape(na, nb, rows, x.shape[1]) for x in arrays] + list(shares)
     results = pl.pallas_call(
         functools.partial(exchange_kernel, (na, nb), widths, forward),
         out_shape=outs,
-        in_specs=[vmem] * len(operands),
+        in_specs=in_specs,
         out_specs=[vmem] * len(outs),
         scratch_shapes=scratch,
         compiler_params=pltpu.CompilerParams(
-            collective_id=ident, has_side_effects=True, vmem_limit_bytes=VMEM_BYTES
+            collective_id=ident, has_side_effects=True,
+            vmem_limit_bytes=(36 if forward else 10) * MIB,
         ),
         name="forward_exchange" if forward else "backward_exchange",
     )(*operands)
@@ -273,21 +329,40 @@
         in_specs=[vmem],
         out_specs=vmem,
         scratch_shapes=[dma, dma((total - 1,)), dma((total - 1,))],
-        compiler_params=pltpu.CompilerParams(collective_id=0, has_side_effects=True),
+        compiler_params=pltpu.CompilerParams(
+            collective_id=0, has_side_effects=True, vmem_limit_bytes=4 * MIB
+        ),
         name="gather_rows",
     )(x)
     return out.reshape(total * x.shape[0], x.shape[1])
 
 
+def down_step(features):
+    return 256 if features % 256 == 0 else features
+
+
 def errors_kernel(
-    sizes, t_ref, a_ref, b_ref, target, a_err, b_err, a_all, b_all, got, s1, r1, s2, r2
+    sizes, hidden, down, a_ref, b_ref, target, a_err, b_err, a_all, b_all, t_ref, got,
+    s1, r1, s2, r2, s3, r3,
 ):
     me, peers, places = hidden_group(sizes)
     sources = (t_ref, a_ref, b_ref)
     copies = []
-    for i, source in enumerate(sources):
+    for i in (1, 2):
         for d, (peer, place) in enumerate(zip(peers, places)):
-            copy = remote(source.at[peer], got.at[d, i], s1.at[d, i], r1.at[d, i], place)
+            copy = remote(sources[i].at[peer], got.at[d, i], s1.at[d, i], r1.at[d, i], place)
+            copy.start()
+            copies.append(copy)
+    total, rows, features = t_ref.shape
+    step = down_step(features)
+    for c in range(features // step):
+        cols = pl.ds(c * step, step)
+        part = matmul(hidden[...], down[:, cols])
+        t_ref[:, :, cols] = part.astype(BF16).reshape(total, rows, step)
+        for d, (peer, place) in enumerate(zip(peers, places)):
+            copy = remote(
+                t_ref.at[peer, :, cols], got.at[d, 0, :, cols], s3.at[d, c], r3.at[d, c], place
+            )
             copy.start()
             copies.append(copy)
     for copy in copies:
@@ -318,9 +393,10 @@
         copy.wait_send()
 
 
-def errors(parts, sizes):
+def errors(hidden, down, parts, sizes):
     total = sizes[0] * sizes[1]
     tokens, features = parts[0].shape
+    pieces = features // down_step(features)
     rows = tokens // total
     vmem = pl.BlockSpec(memory_space=pltpu.VMEM)
     dma = pltpu.SemaphoreType.DMA
@@ -329,46 +405,46 @@
     target, a_err, b_err, a_all, b_all = pl.pallas_call(
         functools.partial(errors_kernel, sizes),
         out_shape=[own, own, own, full, full],
-        in_specs=[vmem] * 3,
+        in_specs=[vmem] * 4,
         out_specs=[vmem] * 5,
         scratch_shapes=[
+            pltpu.VMEM((total, rows, features), BF16),
             pltpu.VMEM((total - 1, 3, rows, features), BF16),
             dma((total - 1, 3)), dma((total - 1, 3)), dma((total - 1, 2)), dma((total - 1, 2)),
+            dma((total - 1, pieces)), dma((total - 1, pieces)),
         ],
         compiler_params=pltpu.CompilerParams(
-            collective_id=1, has_side_effects=True, vmem_limit_bytes=VMEM_BYTES
+            collective_id=1, has_side_effects=True, vmem_limit_bytes=24 * MIB
         ),
         name="errors",
-    )(*[x.reshape(total, rows, features) for x in parts])
+    )(hidden, down, *[x.reshape(total, rows, features) for x in parts])
     return target, a_err, b_err, a_all.reshape(tokens, -1), b_all.reshape(tokens, -1)
 
 
-def outer_kernel(left, gate, up, gate_out, up_out):
-    gate_out[...] = matmul(left[...], gate[...]).astype(BF16)
-    up_out[...] = matmul(left[...], up[...]).astype(BF16)
-
-
-def weight_grads(columns_t, gate, up):
-    features, tokens = columns_t.shape
-    width = gate.shape[1]
-    tile = next((t for t in (256, LANES) if width % t == 0), width)
-    block = pl.BlockSpec((tokens, tile), lambda i: (0, i))
-    out_block = pl.BlockSpec((features, tile), lambda i: (0, i))
-    out = jax.ShapeDtypeStruct((features, width), BF16)
+def outer_kernel(columns, *refs):
+    half = len(refs) // 2
+    left = columns[...].T
+    for grad, out in zip(refs[:half], refs[half:]):
+        out[...] = matmul(left, grad[...]).astype(BF16)
+
+
+def weight_grads(columns, grads):
+    tokens, features = columns.shape
+    tile = LANES
+    out_bytes = 2 * features * sum(g.shape[1] for g in grads)
     return pl.pallas_call(
         outer_kernel,
-        grid=(width // tile,),
-        out_shape=[out, out],
-        in_specs=[pl.BlockSpec((features, tokens), lambda i: (0, 0)), block, block],
-        out_specs=[out_block, out_block],
-        compiler_params=pltpu.CompilerParams(vmem_limit_bytes=VMEM_BYTES),
+        grid=(features // tile,),
+        out_shape=[jax.ShapeDtypeStruct((features, g.shape[1]), BF16) for g in grads],
+        in_specs=[pl.BlockSpec((tokens, tile), lambda i: (0, i))]
+        + [pl.BlockSpec(memory_space=pltpu.VMEM)] * len(grads),
+        out_specs=[pl.BlockSpec((tile, g.shape[1]), lambda i: (i, 0)) for g in grads],
+        compiler_params=pltpu.CompilerParams(vmem_limit_bytes=16 * MIB),
         cost_estimate=pl.CostEstimate(
-            flops=4 * features * tokens * width,
-            bytes_accessed=4 * (features + tokens) * width,
-            transcendentals=0,
+            flops=tokens * out_bytes, bytes_accessed=out_bytes, transcendentals=0
         ),
         name="weight_grads",
-    )(columns_t, gate, up)
+    )(columns, *grads)
 
 
 def body(
@@ -376,15 +452,18 @@
     second_gate, second_up, second_down,
 ):
     columns = gather_rows(inputs, sizes)
-    weights = (parent_gate, parent_up, first_gate, first_up, second_gate, second_up)
+    weights = (first_gate, first_up, second_gate, second_up)
     partials = [matmul(columns, w).astype(BF16) for w in weights]
-    (parent_hidden, first_hidden, second_hidden), kept = exchange(partials, (), tok, True, 2)
+    (parent_hidden, first_hidden, second_hidden), kept = exchange(
+        partials, (), tok, True, 2, (columns, parent_gate, parent_up)
+    )
     outs = [
-        matmul(parent_hidden, parent_down).astype(BF16),
         matmul(first_hidden, first_down).astype(BF16),
         matmul(second_hidden, second_down).astype(BF16),
     ]
-    target, first_error, second_error, first_all, second_all = errors(outs, sizes)
+    target, first_error, second_error, first_all, second_all = errors(
+        parent_hidden, parent_down, outs, sizes
+    )
     backs = [
         outer_cols(first_all, first_down).astype(BF16),
         outer_cols(second_all, second_down).astype(BF16),
@@ -392,9 +471,9 @@
     grads, _ = exchange(backs, kept[2:], tok, False, 3)
     first_grad_down = inner_rows(first_hidden, first_all).astype(BF16)
     second_grad_down = inner_rows(second_hidden, second_all).astype(BF16)
-    columns_t = columns.T
-    first_grad_gate, first_grad_up = weight_grads(columns_t, grads[0], grads[1])
-    second_grad_gate, second_grad_up = weight_grads(columns_t, grads[2], grads[3])
+    first_grad_gate, first_grad_up, second_grad_gate, second_grad_up = weight_grads(
+        columns, grads
+    )
     return (
         target, first_error, second_error,
         first_grad_gate, first_grad_up, first_grad_down,

time: 235 us -> 197 us (0.84)
  matrix products: 33.5 us -> 13.8 us
  Pallas kernels: 189 us -> 179 us
  local copies, waits for them, and re-layouts: 10.5 us -> 3.47 us
    dot_general x9 -> x6, matrix products: 23.4 us -> 5.9 us  [matmul(): return jnp.dot(left, right, preferred_element_type=F32)]
    unnamed x53 -> x23, local copies, waits for them, and re-layouts: 8.73 us -> 3.47 us
    pallas_call x2 -> x1, Pallas kernels: 12.1 us -> 6.96 us  [weight_grads(): pl.pallas_call(outer_kernel, grid=(features // tile,), out_shape=[jax.Sha...]
    pallas_call x2, Pallas kernels: 151 us -> 146 us  [exchange(): pl.pallas_call(functools.partial(exchange_kernel, (na, nb), widths, forwa...]
where the time goes in v2:
time: 197 us
  Pallas kernels  179 us (91%)
  matrix products  13.8 us (7%)
  local copies, waits for them, and re-layouts  3.47 us (2%)
    pallas_call x2, Pallas kernels, exchange(): pl.pallas_call(functools.partial(exchange_kernel, (na, nb), widths, forwa...  146 us
    pallas_call x1, Pallas kernels, errors(): pl.pallas_call(functools.partial(errors_kernel, sizes), out_shape=[own, o...  19.5 us
    pallas_call x1, Pallas kernels, weight_grads(): pl.pallas_call(outer_kernel, grid=(features // tile,), out_shape=[jax.Sha...  6.96 us
    pallas_call x1, Pallas kernels, gather_rows(): pl.pallas_call(functools.partial(gather_kernel, sizes), out_shape=jax.Sha...  6.35 us
    dot_general x6, matrix products, matmul(): return jnp.dot(left, right, preferred_element_type=F32)  5.9 us
    dot_general x2, matrix products, inner_rows(): lax.dot_general(left, right, (((0,), (0,)), ((), ())), preferred_element_...  5.49 us

profile of v2, /device:TPU:0, one launch (start us, length us, event | category | flops | bytes accessed | tf_op | source)
XLA Modules:
  0.0 197.3 jit_solution(2166800906027438357)
XLA Ops:
  0.6 0.0 copy-start
  0.7 0.0 copy-start.1
  0.7 1.0 copy-done.1
  1.6 6.3 %gather_rows.1 = bf16[4,32,1024]{2,1,0:T(8,128)(2,1)S(1)} custom-call(bf16[32,1024]{1,0:T(8,128)(2,1)S(1)} %copy-done.1), custom_call_target="tpu_custom_call" | custom-call | tf_op jit(solution)/shard_map/gather_rows/pallas_call | solution.py:326
  8.0 0.0 copy-start.4
  8.0 2.8 %convolution_convert_fusion.4 = bf16[128,1792]{1,0:T(8,128)(2,1)S(1)} fusion(bf16[128,1024]{1,0:T(8,128)(2,1)S(1)} %bitcast.40, bf16[1024,1792]{1,0:T(8,128)(2,1)} %param.14), kind=kOutput, calls=%fused_computation.4 | convolution fusion | flops 469991424 | bytes 4390912 | tf_op jit(solution)/shard_map/dot_general | solution.py:20
  10.9 0.0 copy-done.3
  10.9 0.0 copy-start.5
  10.9 0.7 convolution_convert_fusion.3
  11.5 0.0 copy-done.4
  11.6 0.6 convolution_convert_fusion.7
  12.2 0.6 copy-done.5
  12.7 0.6 convolution_convert_fusion.6
  13.3 0.0 slice-start
  13.3 0.0 copy-start.2
  13.3 0.0 slice-start.1
  13.3 0.0 slice-start.2
  13.3 0.0 slice-start.3
  13.4 106.2 %forward_exchange.1 = (bf16[4,2,16,7168]{3,2,1,0:T(8,128)(2,1)S(1)}, bf16[4,2,16,1792]{3,2,1,0:T(8,128)(2,1)S(1)}, bf16[4,2,16,1408]{3,2,1,0:T(8,128)(2,1)S(1)},...) custom-call(bf16[128,1024]{1,0:T(8,128)(2,1)S(1)} %bitcast.44, ...), custom_call_target="tpu_custom_call" | custom-call | tf_op jit(solution)/shard_map/forward_exchange/pallas_call | solution.py:276
  119.6 0.0 copy-done.2
  119.6 0.6 convolution_convert_fusion.8
  120.2 0.6 convolution_convert_fusion.9
  120.9 19.5 %errors.1 = (bf16[32,1024]{1,0:T(8,128)(2,1)S(1)}, bf16[32,1024]{1,0:T(8,128)(2,1)S(1)}, bf16[32,1024]{1,0:T(8,128)(2,1)S(1)}, bf16[4,32,1024]{2,1,0:T(8,128)(2,1)S(1)}, bf16[4,32,1024]{2,1,0:T(8,128)(2,1)S(1)}) custom-call(bf16[128,7168]{1,0:T(8,128)(2,1)S(1)} %bitcast.50, bf16[7168,1024]{1,0:T(8,128)(2,1)S(1)} %bitcast.39, ...), custom_call_target="tpu_custom_call" | custom-call | tf_op jit(solution)/shard_map/errors/pallas_call | solution.py:405
  140.4 1.3 convolution_convert_fusion.2
  141.7 1.0 convolution_convert_fusion.5
  142.8 40.1 %backward_exchange.1 = (bf16[4,2,16,1792]{3,2,1,0:T(8,128)(2,1)S(1)}, bf16[4,2,16,1792]{3,2,1,0:T(8,128)(2,1)S(1)}, bf16[4,2,16,1408]{3,2,1,0:T(8,128)(2,1)S(1)}, bf16[4,2,16,1408]{3,2,1,0:T(8,128)(2,1)S(1)}) custom-call(bf16[4,2,16,1792]{3,2,1,0:T(8,128)(2,1)S(1)} %bitcast.51, bf16[4,2,16,1408]{3,2,1,0:T(8,128)(2,1)S(1)} %bitcast.52, ...), custom_call_target="tpu_custom_call" | custom-call | tf_op jit(solution)/shard_map/backward_exchange/pallas_call | solution.py:276
  182.9 7.0 %weight_grads.1 = (bf16[1024,1792]{1,0:T(8,128)(2,1)}, bf16[1024,1792]{1,0:T(8,128)(2,1)}, bf16[1024,1408]{1,0:T(8,128)(2,1)}, bf16[1024,1408]{1,0:T(8,128)(2,1)}) custom-call(bf16[128,1024]{1,0:T(8,128)(2,1)S(1)} %bitcast.45, bf16[128,1792]{1,0:T(8,128)(2,1)S(1)} %bitcast.63, bf16[128,1792]{1,0:T(8,128)(2,1)S(1)} %bitcast.64, ...), custom_call_target="tpu_custom_call" | custom-call | flops 1677721600 | bytes 13107200 | tf_op jit(solution)/shard_map/weight_grads/pallas_call | solution.py:435
  189.9 3.0 %convolution_convert_fusion.1 = bf16[1792,1024]{1,0:T(8,128)(2,1)} fusion(bf16[128,1792]{1,0:T(8,128)(2,1)S(1)} %bitcast.47, bf16[128,1024]{1,0:T(8,128)(2,1)S(1)} %bitcast.60), kind=kOutput, calls=%fused_computation.1 | convolution fusion | flops 471597056 | bytes 4390912 | tf_op jit(solution)/shard_map/dot_general | solution.py:24
  192.9 2.5 %convolution_convert_fusion = bf16[1408,1024]{1,0:T(8,128)(2,1)} fusion(bf16[128,1408]{1,0:T(8,128)(2,1)S(1)} %bitcast.54, bf16[128,1024]{1,0:T(8,128)(2,1)S(1)} %bitcast.62), kind=kOutput, calls=%fused_computation | convolution fusion | flops 370540544 | bytes 3506176 | tf_op jit(solution)/shard_map/dot_general | solution.py:24
  195.4 0.6 copy.22
  196.0 0.6 copy.23
  196.7 0.6 copy.24
  (7 shorter events, 0.0 us)
Async XLA Ops:
  0.6 119.6 %copy-start = (bf16[1408,1024]{1,0:T(8,128)(2,1)S(1)}, bf16[1408,1024]{1,0:T(8,128)(2,1)}, u32[]{:S(2)}) copy-start(bf16[1408,1024]{1,0:T(8,128)(2,1)} %param.19) | copy-start | bytes 8650756
  0.7 1.0 copy-start.1
  1.6 9.2 %copy-start.3 = (bf16[1024,1792]{1,0:T(8,128)(2,1)S(1)}, bf16[1024,1792]{1,0:T(8,128)(2,1)}, u32[]{:S(2)}) copy-start(bf16[1024,1792]{1,0:T(8,128)(2,1)} %param.15) | copy-start | bytes 11010052
  8.0 3.5 %copy-start.4 = (bf16[1024,1408]{1,0:T(8,128)(2,1)S(1)}, bf16[1024,1408]{1,0:T(8,128)(2,1)}, u32[]{:S(2)}) copy-start(bf16[1024,1408]{1,0:T(8,128)(2,1)} %param.17) | copy-start | bytes 8650756
  10.9 1.8 copy-start.5
  13.3 107.5 %slice-start = ((s8[14680064]{0:T(1024)(128)(4,1)}), s8[4194304]{0:T(1024)(128)(4,1)S(1)}, s32[]{:S(2)}) async-start(s8[14680064]{0:T(1024)(128)(4,1)} %bitcast.38), calls=%async_computation | async-start | bytes 8388608
  13.3 106.2 %copy-start.2 = (bf16[1792,1024]{1,0:T(8,128)(2,1)S(1)}, bf16[1792,1024]{1,0:T(8,128)(2,1)}, u32[]{:S(2)}) copy-start(bf16[1792,1024]{1,0:T(8,128)(2,1)} %param.16) | copy-start | bytes 11010052
  13.3 107.5 %slice-start.1 = ((s8[14680064]{0:T(1024)(128)(4,1)}), s8[4194304]{0:T(1024)(128)(4,1)S(1)}, s32[]{:S(2)}) async-start(s8[14680064]{0:T(1024)(128)(4,1)} %bitcast.38), calls=%async_computation.1 | async-start | bytes 8388608
  13.3 107.5 %slice-start.2 = ((s8[14680064]{0:T(1024)(128)(4,1)}), s8[4194304]{0:T(1024)(128)(4,1)S(1)}, s32[]{:S(2)}) async-start(s8[14680064]{0:T(1024)(128)(4,1)} %bitcast.38), calls=%async_computation.2 | async-start | bytes 8388608
  13.3 107.5 %slice-start.3 = ((s8[14680064]{0:T(1024)(128)(4,1)}), s8[2097152]{0:T(1024)(128)(4,1)S(1)}, s32[]{:S(2)}) async-start(s8[14680064]{0:T(1024)(128)(4,1)} %bitcast.38), calls=%async_computation.3 | async-start | bytes 4194304
